TPU v7x, 32 devices: a whole 2x2x4 slice. The times are simulated.
32 devices in a mesh: grp: 2 (over y), row: 4 (over x, core), col: 4 (over z).
Axes of the slice: x: 2, y: 2, z: 4, core: 2. Of those that a mesh axis runs over, the one named last changes fastest.
Arguments:
- programs: bfloat16 [2048, 2048], P(('grp', 'row'), 'col'), parts along dimension 0, may hold values from -6 to 6
- tests: bfloat16 [2048, 2048], P(('grp', 'col'), 'row'), parts along dimension 0, may hold values from -6 to 6
- weight: bfloat16 [2048, 2048], P('col', 'row'), may hold values from -0.125 to 0.125
- labels: int32 [2048, 1024], P(('grp', 'row'), 'col'), parts along dimension 0, may hold values 0 or 1
Outputs:
- grad_programs: bfloat16 [2048, 2048], P(('grp', 'row'), 'col'), parts along dimension 0
- grad_tests: bfloat16 [2048, 2048], P(('grp', 'col'), 'row'), parts along dimension 0
- grad_weight: float32 [4096, 2048], P(('grp', 'col'), 'row'), parts along dimension 0
There are 2 independent parts, one for each index of `grp`. A program takes and returns all parts, laid end to end along the dimension named above; an argument that names none is the same for every part. Nothing has to cross between parts.
All inputs are finite; a program needn't handle non-finite values. No bound on the sum of `labels` on one device may be relied on, other than what follows from the above.
Results may differ from a plain program's by a relative error of at most 0.017.
Values may be sent and summed in bfloat16 or wider, within the bound.
A program may use at most 64 MiB of HBM per device.

v0:
```python
import math
import jax
import jax.numpy as jnp
from jax import lax
from jax.sharding import PartitionSpec as P

E = 2048


def contract(left, right, left_dim, right_dim):
    return lax.dot_general(
        left, right, (((left_dim,), (right_dim,)), ((), ())), preferred_element_type=jnp.float32
    )


def local(programs, tests, weight, labels):
    factor = 1.0 / math.sqrt(E)
    targets = labels.astype(jnp.float32)
    w_rows = lax.all_gather(weight, "row", axis=1, tiled=True)
    share = lax.psum_scatter(
        jnp.dot(programs, w_rows, preferred_element_type=jnp.float32).astype(jnp.bfloat16),
        "col",
        scatter_dimension=0,
        tiled=True,
    )
    projected = lax.all_gather(share, "col", axis=0, tiled=True)
    test_whole = lax.all_gather(tests, "row", axis=1, tiled=True)
    logits = contract(projected, test_whole, 1, 1) * factor
    dlogits = (jax.nn.sigmoid(logits) - targets).astype(jnp.bfloat16)
    partial_sums = jnp.dot(dlogits, test_whole, preferred_element_type=jnp.float32)
    summed = lax.psum(partial_sums.astype(jnp.bfloat16), "col")
    grad_programs = (contract(summed, w_rows, 1, 1) * factor).astype(jnp.bfloat16)
    weight_part = contract(programs, summed, 0, 0) * factor
    test_part = contract(dlogits, projected, 0, 0) * factor
    grad_weight, test_total = (
        lax.psum_scatter(
            weight_part.astype(jnp.bfloat16), "row", scatter_dimension=1, tiled=True
        ).astype(jnp.float32),
        lax.psum_scatter(
            test_part.astype(jnp.bfloat16), "row", scatter_dimension=1, tiled=True
        ).astype(jnp.float32),
    )
    grad_tests = test_total.astype(jnp.bfloat16)
    return (grad_programs, grad_tests, grad_weight)


def solution(mesh):
    placed = (
        P(("grp", "row"), "col"),
        P(("grp", "col"), "row"),
        P("col", "row"),
        P(("grp", "row"), "col"),
    )
    return jax.shard_map(
        local,
        mesh=mesh,
        in_specs=placed,
        out_specs=(P(("grp", "row"), "col"), P(("grp", "col"), "row"), P(("grp", "col"), "row")),
        check_vma=False,
    )
```

profile of v0, /device:TPU:0, one launch (start us, length us, event | category | flops | bytes accessed | tf_op | source)
XLA Modules:
  0.0 236.3 jit_solution(9814701826729110321)
XLA Ops:
  7.2 0.0 all-gather.4.cloned.1.call-start
  7.2 0.7 all-gather.4.cloned.1.call-update
  7.9 0.0 reduce-scatter.4.cloned.1.call-start
  8.0 26.9 %all-gather.4.cloned.1.call-done = bf16[512,2048]{1,0:T(8,128)(2,1)} async-done(((bf16[512,512]{1,0:T(8,128)(2,1)}), bf16[512,2048]{1,0:T(8,128)(2,1)}) %all-gather.4.cloned.1.call-update) | async-done | bytes 2097168 | tf_op jit(solution)/shard_map/all_gather | solution.py:19
  34.9 3.3 %convolution_convert_fusion = bf16[256,2048]{1,0:T(8,128)(2,1)} fusion(bf16[256,512]{1,0:T(8,128)(2,1)S(1)} %copy-done, bf16[512,2048]{1,0:T(8,128)(2,1)} %all-gather.4.cloned.1.call-done), kind=kOutput, calls=%fused_computation.3 | convolution fusion | flops 537395200 | bytes 3407872 | tf_op jit(solution)/shard_map/dot_general | solution.py:21
  38.2 0.0 all-gather.8.cloned.1.call-start
  38.2 0.7 all-gather.8.cloned.1.call-update
  38.9 0.0 all-gather.6.cloned.1.call-start
  39.0 26.5 %reduce-scatter.4.cloned.1.call-done = bf16[64,2048]{1,0:T(8,128)(2,1)} async-done(((bf16[256,2048]{1,0:T(8,128)(2,1)}), bf16[64,2048]{1,0:T(8,128)(2,1)}) %reduce-scatter.4.cloned.1.call-update) | async-done | bytes 262160 | tf_op jit(solution)/shard_map/reduce_scatter | solution.py:20
  65.5 0.0 all-reduce.2.cloned.1.call-start
  65.6 17.0 %all-gather.8.cloned.1.call-done = bf16[256,2048]{1,0:T(8,128)(2,1)} async-done(((bf16[256,512]{1,0:T(8,128)(2,1)}), bf16[256,2048]{1,0:T(8,128)(2,1)}) %all-gather.8.cloned.1.call-update) | async-done | bytes 1048592 | tf_op jit(solution)/shard_map/all_gather | solution.py:27
  82.6 29.5 %all-gather.6.cloned.1.call-done = bf16[256,2048]{1,0:T(8,128)(2,1)} async-done(((bf16[64,2048]{1,0:T(8,128)(2,1)}), bf16[256,2048]{1,0:T(8,128)(2,1)}) %all-gather.6.cloned.1.call-update) | async-done | bytes 1048592 | tf_op jit(solution)/shard_map/all_gather | solution.py:26
  112.0 2.0 fusion.8
  114.1 1.4 convolution_convert_fusion.1
  115.5 0.0 reduce-scatter.8.cloned.1.call-start
  115.6 51.4 %all-reduce.2.cloned.1.call-done = bf16[256,2048]{1,0:T(8,128)(2,1)} async-done(((bf16[256,2048]{1,0:T(8,128)(2,1)}), bf16[256,2048]{1,0:T(8,128)(2,1)}) %all-reduce.2.cloned.1.call-update) | async-done | bytes 1048592 | tf_op jit(solution)/shard_map/psum | solution.py:31
  167.0 3.3 %fusion = bf16[512,2048]{0,1:T(8,128)(2,1)} fusion(bf16[256,2048]{1,0:T(8,128)(2,1)} %all-reduce.2.cloned.1.call-done, bf16[256,512]{1,0:T(8,128)(2,1)S(1)} %copy-done), kind=kOutput, calls=%fused_computation.1 | convolution fusion | flops 538968064 | bytes 3407872 | tf_op jit(solution)/shard_map/dot_general | solution.py:11
  170.3 0.0 reduce-scatter.6.cloned.1.call-start
  170.4 1.1 copy-done.2
  171.5 1.4 fusion.1
  173.0 2.7 %fusion.2 = bf16[256,512]{1,0:T(8,128)(2,1)} fusion(bf16[256,2048]{1,0:T(8,128)(2,1)} %all-reduce.2.cloned.1.call-done, bf16[512,2048]{1,0:T(8,128)(2,1)S(1)} %copy-done.1), kind=kOutput, calls=%fused_computation.7 | convolution fusion | flops 537133056 | bytes 3407872 | tf_op jit(solution)/shard_map/dot_general | solution.py:11
  175.6 25.6 %reduce-scatter.8.cloned.1.call-done = bf16[512,512]{0,1:T(8,128)(2,1)} async-done(((bf16[512,2048]{0,1:T(8,128)(2,1)}), bf16[512,512]{0,1:T(8,128)(2,1)}) %reduce-scatter.8.cloned.1.call-update) | async-done | bytes 524304 | tf_op jit(solution)/shard_map/reduce_scatter | solution.py:36
  201.3 2.2 copy.7
  203.5 25.9 %reduce-scatter.6.cloned.1.call-done = bf16[256,512]{1,0:T(8,128)(2,1)} async-done(((bf16[256,2048]{1,0:T(8,128)(2,1)}), bf16[256,512]{1,0:T(8,128)(2,1)}) %reduce-scatter.6.cloned.1.call-update) | async-done | bytes 262160 | tf_op jit(solution)/shard_map/reduce_scatter | solution.py:39
  (14 shorter events, 0.1 us)
Async XLA Ops:
  7.2 27.7 %copy-start = (bf16[256,512]{1,0:T(8,128)(2,1)S(1)}, bf16[256,512]{1,0:T(8,128)(2,1)}, u32[]{:S(2)}) copy-start(bf16[256,512]{1,0:T(8,128)(2,1)} %param.4) | copy-start | bytes 786436
  7.2 27.7 %all-gather.4.cloned.1.call-start = ((), (), s32[]{:S(2)}) async-start(), calls=%async_computation.3 | async-start | bytes 2621440 | tf_op jit(solution)/shard_map/all_gather | solution.py:19
  7.9 104.1 %copy-start.4 = (s32[256,256]{1,0:T(8,128)S(1)}, s32[256,256]{1,0:T(8,128)}, u32[]{:S(2)}) copy-start(s32[256,256]{1,0:T(8,128)} %param.7) | copy-start | bytes 786436
  7.9 57.6 %reduce-scatter.4.cloned.1.call-start = ((), (), s32[]{:S(2)}) async-start(), calls=%async_computation.4 | async-start | bytes 1310720 | tf_op jit(solution)/shard_map/reduce_scatter | solution.py:20
  38.2 44.4 %all-gather.8.cloned.1.call-start = ((), (), s32[]{:S(2)}) async-start(), calls=%async_computation.6 | async-start | bytes 1310720 | tf_op jit(solution)/shard_map/all_gather | solution.py:27
  38.9 73.1 %all-gather.6.cloned.1.call-start = ((), (), s32[]{:S(2)}) async-start(), calls=%async_computation.5 | async-start | bytes 1310720 | tf_op jit(solution)/shard_map/all_gather | solution.py:26
  65.5 101.5 %all-reduce.2.cloned.1.call-start = ((), (), s32[]{:S(2)}) async-start(), calls=%async_computation.7 | async-start | bytes 2097152 | tf_op jit(solution)/shard_map/psum | solution.py:31
  82.5 31.5 %copy-start.3 = (bf16[256,2048]{1,0:T(8,128)(2,1)S(1)}, bf16[256,2048]{1,0:T(8,128)(2,1)}, u32[]{:S(2)}) copy-start(bf16[256,2048]{1,0:T(8,128)(2,1)} %all-gather.8.cloned.1.call-done) | copy-start | bytes 3145732
  115.5 85.7 %reduce-scatter.8.cloned.1.call-start = ((), (), s32[]{:S(2)}) async-start(), calls=%async_computation.9 | async-start | bytes 2621440 | tf_op jit(solution)/shard_map/reduce_scatter | solution.py:36
  170.3 1.2 copy-start.2
  170.3 2.7 %copy-start.1 = (bf16[512,2048]{1,0:T(8,128)(2,1)S(1)}, bf16[512,2048]{1,0:T(8,128)(2,1)}, u32[]{:S(2)}) copy-start(bf16[512,2048]{1,0:T(8,128)(2,1)} %all-gather.4.cloned.1.call-done) | copy-start | bytes 6291460
  170.3 59.1 %reduce-scatter.6.cloned.1.call-start = ((), (), s32[]{:S(2)}) async-start(), calls=%async_computation.8 | async-start | bytes 1310720 | tf_op jit(solution)/shard_map/reduce_scatter | solution.py:39
Sparse Core Ops, SparseCore 0:
  9.6 25.2 all-gather.3
  38.3 27.1 reduce-scatter.3
  67.1 15.3 all-gather.7
  84.1 27.9 all-gather.5
  115.6 51.3 all-reduce.1
  170.4 30.7 reduce-scatter.7
  204.5 24.8 reduce-scatter.5
where the time goes:
time: 237 us; the launch traced here: 236 us
  waiting for transfers between devices  204 us (86%)
  between operations  14.2 us (6%)
  matrix products  14.1 us (6%)
  local copies, waits for them, and re-layouts  3.38 us (1%)
    psum x1, waiting for transfers between devices, local(): summed = lax.psum(partial_sums.astype(jnp.bfloat16), 'col')  51.4 us
    all_gather x1, waiting for transfers between devices, local(): projected = lax.all_gather(share, 'col', axis=0, tiled=True)  29.5 us
    all_gather x1, waiting for transfers between devices, local(): w_rows = lax.all_gather(weight, 'row', axis=1, tiled=True)  26.9 us
    reduce_scatter x1, waiting for transfers between devices, local(): lax.psum_scatter(jnp.dot(programs, w_rows, preferred_element_type=jnp.flo...  26.5 us
    reduce_scatter x1, waiting for transfers between devices, local(): lax.psum_scatter(test_part.astype(jnp.bfloat16), 'row', scatter_dimension...  25.9 us
    reduce_scatter x1, waiting for transfers between devices, local(): lax.psum_scatter(weight_part.astype(jnp.bfloat16), 'row', scatter_dimensi...  25.6 us
    all_gather x1, waiting for transfers between devices, local(): test_whole = lax.all_gather(tests, 'row', axis=1, tiled=True)  17 us
    dot_general x4, matrix products, contract(): lax.dot_general(left, right, (((left_dim,), (right_dim,)), ((), ())), pre...  9.44 us
  transfers between devices with their start and end apart: 7, of which 7 were waited for; matrix products, arithmetic and copies ran while one was open for 3% of the time, Pallas kernels for 0%

commit v1 on v0

--- a/solution.py
+++ b/solution.py
@@ -28,7 +28,7 @@
     logits = contract(projected, test_whole, 1, 1) * factor
     dlogits = (jax.nn.sigmoid(logits) - targets).astype(jnp.bfloat16)
     partial_sums = jnp.dot(dlogits, test_whole, preferred_element_type=jnp.float32)
-    summed = lax.psum(partial_sums.astype(jnp.bfloat16), "col")
+    summed = jnp.sum(lax.all_gather(partial_sums.astype(jnp.bfloat16), "col"), axis=0)
     grad_programs = (contract(summed, w_rows, 1, 1) * factor).astype(jnp.bfloat16)
     weight_part = contract(programs, summed, 0, 0) * factor
     test_part = contract(dlogits, projected, 0, 0) * factor

time: 237 us -> 266 us (1.12)
  waiting for transfers between devices: 204 us -> 232 us
  other arithmetic: 0 us -> 3.07 us
    all_gather x0 -> x1, waiting for transfers between devices: none -> 80.4 us  [local(): lax.all_gather(partial_sums.astype(jnp.bfloat16), 'col')]
    psum x1 -> x0, waiting for transfers between devices: 51.4 us -> none  [local(): summed = lax.psum(partial_sums.astype(jnp.bfloat16), 'col')]
    reduce_sum x0 -> x1, other arithmetic: none -> 3.07 us  [local(): jnp.sum(lax.all_gather(partial_sums.astype(jnp.bfloat16), 'col'), axis=0)]
  transfers between devices with their start and end apart: 7 -> 7, of which waited for: 7 -> 7; matrix products, arithmetic and copies ran while one was open for 3% -> 2% of each run, Pallas kernels for 0% -> 0%
where the time goes in v1:
time: 266 us
  waiting for transfers between devices  232 us (87%)
  between operations  14.2 us (5%)
  matrix products  12.9 us (5%)
  local copies, waits for them, and re-layouts  3.39 us (1%)
  other arithmetic  3.07 us (1%)
    all_gather x1, waiting for transfers between devices, local(): lax.all_gather(partial_sums.astype(jnp.bfloat16), 'col')  80.4 us
    all_gather x1, waiting for transfers between devices, local(): projected = lax.all_gather(share, 'col', axis=0, tiled=True)  29.5 us
    all_gather x1, waiting for transfers between devices, local(): w_rows = lax.all_gather(weight, 'row', axis=1, tiled=True)  26.9 us
    reduce_scatter x1, waiting for transfers between devices, local(): lax.psum_scatter(jnp.dot(programs, w_rows, preferred_element_type=jnp.flo...  26.5 us
    reduce_scatter x1, waiting for transfers between devices, local(): lax.psum_scatter(test_part.astype(jnp.bfloat16), 'row', scatter_dimension...  25.8 us
    reduce_scatter x1, waiting for transfers between devices, local(): lax.psum_scatter(weight_part.astype(jnp.bfloat16), 'row', scatter_dimensi...  24.8 us
    all_gather x1, waiting for transfers between devices, local(): test_whole = lax.all_gather(tests, 'row', axis=1, tiled=True)  17 us
    dot_general x4, matrix products, contract(): lax.dot_general(left, right, (((left_dim,), (right_dim,)), ((), ())), pre...  8.23 us
  transfers between devices with their start and end apart: 7, of which 7 were waited for; matrix products, arithmetic and copies ran while one was open for 2% of the time, Pallas kernels for 0%

profile of v1, /device:TPU:0, one launch (start us, length us, event | category | flops | bytes accessed | tf_op | source)
XLA Modules:
  0.0 266.1 jit_solution(17108373840968696507)
XLA Ops:
  7.2 0.7 all-gather.6.cloned.1.call-update
  7.9 0.0 reduce-scatter.4.cloned.1.call-start
  8.0 26.9 %all-gather.6.cloned.1.call-done = bf16[512,2048]{1,0:T(8,128)(2,1)} async-done(((bf16[512,512]{1,0:T(8,128)(2,1)}), bf16[512,2048]{1,0:T(8,128)(2,1)}) %all-gather.6.cloned.1.call-update) | async-done | bytes 2097168 | tf_op jit(solution)/shard_map/all_gather | solution.py:19
  34.9 3.3 %convolution_convert_fusion = bf16[256,2048]{1,0:T(8,128)(2,1)} fusion(bf16[256,512]{1,0:T(8,128)(2,1)S(1)} %copy-done, bf16[512,2048]{1,0:T(8,128)(2,1)} %all-gather.6.cloned.1.call-done), kind=kOutput, calls=%fused_computation.3 | convolution fusion | flops 537395200 | bytes 3407872 | tf_op jit(solution)/shard_map/dot_general | solution.py:21
  38.2 0.0 all-gather.10.cloned.1.call-start
  38.2 0.7 all-gather.10.cloned.1.call-update
  38.9 0.0 all-gather.8.cloned.1.call-start
  39.0 26.5 %reduce-scatter.4.cloned.1.call-done = bf16[64,2048]{1,0:T(8,128)(2,1)} async-done(((bf16[256,2048]{1,0:T(8,128)(2,1)}), bf16[64,2048]{1,0:T(8,128)(2,1)}) %reduce-scatter.4.cloned.1.call-update) | async-done | bytes 262160 | tf_op jit(solution)/shard_map/reduce_scatter | solution.py:20
  65.5 0.0 all-gather.12.cloned.1.call-start
  65.6 17.0 %all-gather.10.cloned.1.call-done = bf16[256,2048]{1,0:T(8,128)(2,1)} async-done(((bf16[256,512]{1,0:T(8,128)(2,1)}), bf16[256,2048]{1,0:T(8,128)(2,1)}) %all-gather.10.cloned.1.call-update) | async-done | bytes 1048592 | tf_op jit(solution)/shard_map/all_gather | solution.py:27
  82.6 29.5 %all-gather.8.cloned.1.call-done = bf16[256,2048]{1,0:T(8,128)(2,1)} async-done(((bf16[64,2048]{1,0:T(8,128)(2,1)}), bf16[256,2048]{1,0:T(8,128)(2,1)}) %all-gather.8.cloned.1.call-update) | async-done | bytes 1048592 | tf_op jit(solution)/shard_map/all_gather | solution.py:26
  112.0 2.0 fusion.8
  114.1 1.4 convolution_convert_fusion.1
  115.5 0.0 reduce-scatter.8.cloned.1.call-start
  115.6 80.4 %all-gather.12.cloned.1.call-done = bf16[1024,2048]{1,0:T(8,128)(2,1)} async-done(((bf16[256,2048]{1,0:T(8,128)(2,1)}), bf16[1024,2048]{1,0:T(8,128)(2,1)}) %all-gather.12.cloned.1.call-update) | async-done | bytes 4194320 | tf_op jit(solution)/shard_map/all_gather | solution.py:31
  195.9 3.1 %reduce_sum.12 = bf16[256,2048]{1,0:T(8,128)(2,1)S(1)} reduce(bf16[4,256,2048]{2,1,0:T(8,128)(2,1)} %bitcast.15, bf16[]{:T(256)} %constant.5.clone.1), dimensions={0}, to_apply=%region_1.0 | reduce | flops 1572864 | bytes 5242882 | tf_op jit(solution)/shard_map/reduce_sum | solution.py:31
  199.0 2.1 fusion
  201.1 0.0 reduce-scatter.6.cloned.1.call-start
  201.2 1.1 copy-done.2
  202.3 1.4 fusion.1
  203.8 2.7 %fusion.2 = bf16[256,512]{1,0:T(8,128)(2,1)} fusion(bf16[256,2048]{1,0:T(8,128)(2,1)} %copy-done.4, bf16[512,2048]{1,0:T(8,128)(2,1)S(1)} %copy-done.1), kind=kOutput, calls=%fused_computation.7 | convolution fusion | flops 537133056 | bytes 3407872 | tf_op jit(solution)/shard_map/dot_general | solution.py:11
  206.5 24.8 %reduce-scatter.8.cloned.1.call-done = bf16[512,512]{0,1:T(8,128)(2,1)} async-done(((bf16[512,2048]{0,1:T(8,128)(2,1)}), bf16[512,512]{0,1:T(8,128)(2,1)}) %reduce-scatter.8.cloned.1.call-update) | async-done | bytes 524304 | tf_op jit(solution)/shard_map/reduce_scatter | solution.py:36
  231.2 2.2 copy.7
  233.4 25.8 %reduce-scatter.6.cloned.1.call-done = bf16[256,512]{1,0:T(8,128)(2,1)} async-done(((bf16[256,2048]{1,0:T(8,128)(2,1)}), bf16[256,512]{1,0:T(8,128)(2,1)}) %reduce-scatter.6.cloned.1.call-update) | async-done | bytes 262160 | tf_op jit(solution)/shard_map/reduce_scatter | solution.py:39
  (17 shorter events, 0.1 us)
Async XLA Ops:
  7.2 27.7 %copy-start = (bf16[256,512]{1,0:T(8,128)(2,1)S(1)}, bf16[256,512]{1,0:T(8,128)(2,1)}, u32[]{:S(2)}) copy-start(bf16[256,512]{1,0:T(8,128)(2,1)} %param.4) | copy-start | bytes 786436
  7.2 27.7 %all-gather.6.cloned.1.call-start = ((), (), s32[]{:S(2)}) async-start(), calls=%async_computation.3 | async-start | bytes 2621440 | tf_op jit(solution)/shard_map/all_gather | solution.py:19
  7.9 104.1 %copy-start.5 = (s32[256,256]{1,0:T(8,128)S(1)}, s32[256,256]{1,0:T(8,128)}, u32[]{:S(2)}) copy-start(s32[256,256]{1,0:T(8,128)} %param.7) | copy-start | bytes 786436
  7.9 57.6 %reduce-scatter.4.cloned.1.call-start = ((), (), s32[]{:S(2)}) async-start(), calls=%async_computation.4 | async-start | bytes 1310720 | tf_op jit(solution)/shard_map/reduce_scatter | solution.py:20
  38.2 44.4 %all-gather.10.cloned.1.call-start = ((), (), s32[]{:S(2)}) async-start(), calls=%async_computation.6 | async-start | bytes 1310720 | tf_op jit(solution)/shard_map/all_gather | solution.py:27
  38.9 73.1 %all-gather.8.cloned.1.call-start = ((), (), s32[]{:S(2)}) async-start(), calls=%async_computation.5 | async-start | bytes 1310720 | tf_op jit(solution)/shard_map/all_gather | solution.py:26
  65.5 130.4 %all-gather.12.cloned.1.call-start = ((), (), s32[]{:S(2)}) async-start(), calls=%async_computation.9 | async-start | bytes 5242880 | tf_op jit(solution)/shard_map/all_gather | solution.py:31
  82.5 31.5 %copy-start.3 = (bf16[256,2048]{1,0:T(8,128)(2,1)S(1)}, bf16[256,2048]{1,0:T(8,128)(2,1)}, u32[]{:S(2)}) copy-start(bf16[256,2048]{1,0:T(8,128)(2,1)} %all-gather.10.cloned.1.call-done) | copy-start | bytes 3145732
  115.5 115.7 %reduce-scatter.8.cloned.1.call-start = ((), (), s32[]{:S(2)}) async-start(), calls=%async_computation.8 | async-start | bytes 2621440 | tf_op jit(solution)/shard_map/reduce_scatter | solution.py:36
  199.0 2.1 copy-start.4
  201.1 1.2 copy-start.2
  201.1 2.7 copy-start.1
  201.1 58.1 %reduce-scatter.6.cloned.1.call-start = ((), (), s32[]{:S(2)}) async-start(), calls=%async_computation.7 | async-start | bytes 1310720 | tf_op jit(solution)/shard_map/reduce_scatter | solution.py:39
Sparse Core Ops, SparseCore 0:
  9.6 25.2 all-gather.5
  38.3 27.1 reduce-scatter.3
  67.1 15.3 all-gather.9
  84.1 27.9 all-gather.7
  115.6 80.2 all-gather.11
  201.2 29.9 reduce-scatter.7
  234.3 24.8 reduce-scatter.5
